TPU v7x, 512 devices: a whole 4x4x16 slice. The times are simulated.
512 devices in a mesh: lat: 32 (over z, core), ch: 16 (over y, x).
Axes of the slice: x: 4, y: 4, z: 16, core: 2. Of those that a mesh axis runs over, the one named last changes fastest.
Arguments:
- fields: bfloat16 [2, 704, 32, 1440], P(None, 'lat', 'ch'), may hold values from -6 to 6
- table: bfloat16 [704, 704, 352], P('lat', 'ch'), may hold values from -1 to 1, as said below
Outputs:
- coefficients: float32 [704, 704, 128], P('lat', 'ch')
Inputs may be any that keep to these rules, and one draw needn't show every extreme that they name: table[m, l, k] is zero wherever l < m.
All inputs are finite; a program needn't handle non-finite values.
Results may differ from a plain program's by a relative error of at most 0.005.
Values may be sent and summed in bfloat16 or wider, within the bound.
A program may use at most 64 MiB of HBM per device.

v0:
```python
import math
import jax
import jax.numpy as jnp
from jax import lax
from jax.sharding import PartitionSpec as P

MODES = 704


def fourier_table(nlon, modes):
    cols = jnp.arange(nlon, dtype=jnp.int32)[:, None]
    orders = jnp.arange(modes, dtype=jnp.int32)[None, :]
    phase = (cols * orders % nlon).astype(jnp.float32) * (2.0 * math.pi / nlon)
    factor = 1.0 / math.sqrt(nlon)
    return jnp.concatenate([jnp.cos(phase) * factor, -jnp.sin(phase) * factor], axis=1).astype(
        jnp.bfloat16
    )


def parity_project(block, parts, order_start, degree_start):
    order_count, degree_count, hemisphere = block.shape
    padding = degree_count % 2
    first_rows = block[:, 0::2]
    second_rows = block[:, 1::2]
    orders = order_start + jnp.arange(order_count, dtype=jnp.int32)[:, None, None]
    aligned = (degree_start - orders) % 2 == 0
    sym_table = jnp.where(aligned, first_rows, second_rows)
    anti_table = jnp.where(aligned, second_rows, first_rows)
    sym_coeffs = jnp.einsum(
        "mlk,bkcrm->mlbcr", sym_table, parts[:, :hemisphere], preferred_element_type=jnp.float32
    )
    anti_coeffs = jnp.einsum(
        "mlk,bkcrm->mlbcr", anti_table, parts[:, hemisphere:], preferred_element_type=jnp.float32
    )
    chosen = aligned[:, :, :, None, None]
    first_out = jnp.where(chosen, sym_coeffs, anti_coeffs)
    second_out = jnp.where(chosen, anti_coeffs, sym_coeffs)
    joined = jnp.stack([first_out, second_out], axis=2)
    joined = joined.reshape((order_count, degree_count + padding) + sym_coeffs.shape[2:])
    return joined


def shards(fields, table):
    batch, rows, chans, nlon = fields.shape
    slab, lblock, half = table.shape
    fourier = fourier_table(nlon, MODES)
    spectrum = jnp.einsum("brcj,jn->brcn", fields, fourier, preferred_element_type=jnp.float32)
    spectrum = spectrum.astype(jnp.bfloat16).reshape(batch, rows, chans, 2, MODES)
    moved = lax.all_to_all(spectrum, "lat", split_axis=4, concat_axis=1, tiled=True)
    north = moved[:, :half].astype(jnp.float32)
    south = moved[:, half:][:, ::-1].astype(jnp.float32)
    parts = jnp.concatenate(
        [(north + south).astype(jnp.bfloat16), (north - south).astype(jnp.bfloat16)], axis=1
    )
    order_start = lax.axis_index("lat") * slab
    degree_start = lax.axis_index("ch") * lblock
    gathered = parity_project(
        table, lax.all_gather(parts, "ch", axis=2, tiled=True), order_start, degree_start
    )
    return gathered.reshape(slab, lblock, -1)


def solution(mesh):
    return jax.shard_map(
        shards,
        mesh=mesh,
        in_specs=(P(None, "lat", "ch", None), P("lat", "ch", None)),
        out_specs=P("lat", "ch", None),
        check_vma=False,
    )
```

profile of v0, /device:TPU:1, one launch (start us, length us, event | category | flops | bytes accessed | tf_op | source)
XLA Modules:
  0.0 162.0 jit_solution(14036317072984009875)
XLA Ops:
  6.5 0.0 copy-start
  6.5 0.0 all-gather.2.cloned.1.call-start
  6.5 19.1 %multiply_convert_fusion = (bf16[1440,704]{1,0:T(8,128)(2,1)S(1)}, bf16[1440,704]{1,0:T(8,128)(2,1)S(1)}) fusion(), kind=kLoop, calls=%fused_computation.3 | loop fusion | flops 14192640 | bytes 4055040 | tf_op jit(solution)/shard_map/convert.1
  25.7 0.0 copy-done
  25.7 1.0 fusion.7
  26.7 0.3 reshape.50
  27.0 1.8 %copy.24 = bf16[2,22,2,2,704]{1,3,2,0,4:T(2,128)(2,1)S(1)} copy(bf16[2,22,2,2,704]{4,3,1,2,0:T(2,128)(2,1)S(1)} %reshape.50) | data formatting | bytes 495616 | tf_op jit(solution)/shard_map/reshape | solution.py:48
  28.8 1.8 %reshape.51 = bf16[32,2,1936]{2,1,0:T(2,128)(2,1)S(1)} reshape(bf16[704,2,2,2,22]{4,3,2,1,0:T(2,128)(2,1)S(1)} %bitcast.45) | data formatting | bytes 495616
  30.6 38.8 %all_to_all.18 = bf16[32,2,1936]{2,1,0:T(2,128)(2,1)S(1)} all-to-all(bf16[32,2,1936]{2,1,0:T(2,128)(2,1)S(1)} %reshape.51), channel_id=1, replica_groups=mesh['lat'=32,'ch'=16] {'lat'}, dimensions={0} | all-to-all | bytes 495616 | tf_op jit(solution)/shard_map/all_to_all | solution.py:49
  69.5 1.8 %reshape.52 = bf16[704,2,2,2,22]{4,3,2,1,0:T(2,128)(2,1)S(1)} reshape(bf16[32,2,1936]{2,1,0:T(2,128)(2,1)S(1)} %all_to_all.18) | data formatting | bytes 495616
  71.3 0.4 copy.50
  71.7 0.0 copy-start.1
  71.7 2.9 %all_to_all.16 = bf16[2,704,2,2,22]{1,3,4,2,0:T(2,128)(2,1)S(1)} reshape(bf16[2,32,22,2,2,22]{2,1,4,5,3,0:T(8,128)(2,1)S(1)} %bitcast.44) | data formatting | bytes 495616 | tf_op jit(solution)/shard_map/all_to_all | solution.py:49
  74.6 0.0 copy-start.2
  74.6 0.2 slice.25
  74.9 0.8 reverse
  75.7 0.3 fusion.19
  76.0 0.1 fusion.20
  76.1 0.4 pad_maximum_fusion.1
  76.5 0.9 copy.27
  77.4 0.0 all-gather.2.cloned.1.call-update
  77.5 0.0 copy-done.1
  77.5 1.0 slice.18
  78.5 0.0 copy-done.2
  78.5 1.0 slice.19
  79.6 56.5 %all-gather.2.cloned.1.call-done = bf16[2,704,32,2,22]{1,3,4,0,2:T(2,128)(2,1)} async-done(((bf16[2,704,2,2,22]{1,3,4,0,2:T(2,128)(2,1)}), bf16[2,704,32,2,22]{1,3,4,0,2:T(2,128)(2,1)}) %all-gather.2.cloned.1.call-update) | async-done | bytes 3964944 | tf_op jit(solution)/shard_map/all_gather | solution.py:58
  136.1 6.5 %fusion.24 = (bf16[2,352,32,2,22]{1,3,4,0,2:T(2,128)(2,1)S(1)}, bf16[2,352,32,2,22]{1,3,4,0,2:T(2,128)(2,1)S(1)}) fusion(bf16[2,704,32,2,22]{1,3,4,0,2:T(2,128)(2,1)} %all-gather.2.cloned.1.call-done), kind=kLoop, calls=%fused_computation.39 | loop fusion | bytes 7929856 | tf_op jit(solution)/shard_map/slice | solution.py:30
  142.6 2.0 %fusion.8 = f32[22,22,2,32,2]{3,1,4,2,0:T(8,128)S(1)} fusion(bf16[2,352,32,2,22]{1,3,4,0,2:T(2,128)(2,1)S(1)} %get-tuple-element.8, bf16[22,22,352]{2,1,0:T(8,128)(2,1)S(1)} %slice.19, bf16[22,22,352]{2,1,0:T(8,128)(2,1)S(1)} %slice.18, pred[22]{0:T(512)(128)(4,1)S(1)} %fusion.21), kind=kOutput, calls=%fused_computation.14 | convolution fusion | flops 43784576 | bytes 2911766 | tf_op jit(solution)/shard_map/mlk,bkcrm->mlbcr/dot_general | solution.py:32
  144.6 2.0 %select_bitcast_fusion.1 = (f32[22,22,1,2,32,2]{4,1,5,3,0,2:T(8,128)S(1)}, f32[22,22,1,2,32,2]{4,1,5,3,0,2:T(8,128)S(1)}) fusion(f32[22,22,2,32,2]{3,1,4,2,0:T(8,128)S(1)} %fusion.8, pred[22]{0:T(512)(128)(4,1)S(1)} %fusion.21, bf16[2,352,32,2,22]{1,3,4,0,2:T(2,128)(2,1)S(1)} %get-tuple-element.7, bf16[22,22,352]{2,1,0:T(8,128)(2,1)S(1)} %slice.18, ...), kind=kOutput, calls=%fused_computation.20 | convolution fusion | flops 43908480 | bytes 3407382 | tf_op jit(solution)/shard_map/mlk,bkcrm->mlbcr/dot_general | solution.py:29
  146.6 1.6 pad_maximum_fusion
  148.2 5.0 %copy.30 = f32[22,22,2,2,32,2]{0,5,4,3,2,1:T(2,128)S(1)} copy(f32[22,22,2,2,32,2]{4,1,5,3,0,2:T(8,128)} %pad_maximum_fusion) | data formatting | bytes 991232 | tf_op jit(solution)/shard_map/stack | solution.py:38
  153.3 1.9 %copy.31 = f32[22,44,128]{2,1,0:T(8,128)} copy(f32[22,44,128]{0,2,1:T(8,128)S(1)} %bitcast.42) | data formatting | bytes 991232 | tf_op jit(solution)/shard_map/reshape;reshape | solution.py:60
  (1 shorter events, 0.0 us)
Async XLA Ops:
  6.5 19.1 %copy-start = (bf16[2,22,2,1440]{3,2,1,0:T(2,128)(2,1)S(1)}, bf16[2,22,2,1440]{3,2,1,0:T(2,128)(2,1)}, u32[]{:S(2)}) copy-start(bf16[2,22,2,1440]{3,2,1,0:T(2,128)(2,1)} %param.2) | copy-start | bytes 760324
  6.5 129.5 %all-gather.2.cloned.1.call-start = ((), (), s32[]{:S(2)}) async-start(), calls=%async_computation.1 | async-start | bytes 4595712 | tf_op jit(solution)/shard_map/all_gather | solution.py:58
  71.7 5.8 %copy-start.1 = (bf16[22,44,352]{2,1,0:T(8,128)(2,1)S(1)}, bf16[22,44,352]{2,1,0:T(8,128)(2,1)}, u32[]{:S(2)}) copy-start(bf16[22,44,352]{2,1,0:T(8,128)(2,1)} %param.3) | copy-start | bytes 2044420
  74.6 3.9 %copy-start.2 = (bf16[22,44,352]{2,1,0:T(8,128)(2,1)S(1)}, bf16[22,44,352]{2,1,0:T(8,128)(2,1)}, u32[]{:S(2)}) copy-start(bf16[22,44,352]{2,1,0:T(8,128)(2,1)} %param.3) | copy-start | bytes 2044420
Sparse Core Ops, SparseCore 0:
  77.6 58.4 all-gather.1
where the time goes:
time: 162 us
  waiting for transfers between devices  56.5 us (35%)
  blocking collectives  38.8 us (24%)
  local copies, waits for them, and re-layouts  26.6 us (16%)
  other arithmetic  21.5 us (13%)
  between operations  13.6 us (8%)
  matrix products  5.07 us (3%)
    all_gather x1, waiting for transfers between devices, shards(): lax.all_gather(parts, 'ch', axis=2, tiled=True)  56.5 us
    all_to_all x1, blocking collectives, shards(): lax.all_to_all(spectrum, 'lat', split_axis=4, concat_axis=1, tiled=True)  38.8 us
    another operation x1, other arithmetic  19.1 us
    slice x1, local copies, waits for them, and re-layouts, parity_project(): parts[:, :hemisphere]  6.52 us
    another operation x1, local copies, waits for them, and re-layouts, parity_project(): joined = jnp.stack([first_out, second_out], axis=2)  5.04 us
    unnamed x9, local copies, waits for them, and re-layouts  4.41 us
    all_to_all x2, local copies, waits for them, and re-layouts, shards(): lax.all_to_all(spectrum, 'lat', split_axis=4, concat_axis=1, tiled=True)  3.34 us
  transfers between devices with their start and end apart: 1, of which 1 were waited for; matrix products, arithmetic and copies ran while one was open for 1% of the time, Pallas kernels for 0%

commit v1 on v0

--- a/solution.py
+++ b/solution.py
@@ -5,6 +5,11 @@
 from jax.sharding import PartitionSpec as P
 
 MODES = 704
+
+
+def swapped_in(block, axis, along):
+    stack = jnp.stack([block] * lax.axis_size(axis))
+    return jnp.concatenate(lax.all_to_all(stack, axis, 0, 0), axis=along)
 
 
 def fourier_table(nlon, modes):
@@ -54,9 +59,7 @@
     )
     order_start = lax.axis_index("lat") * slab
     degree_start = lax.axis_index("ch") * lblock
-    gathered = parity_project(
-        table, lax.all_gather(parts, "ch", axis=2, tiled=True), order_start, degree_start
-    )
+    gathered = parity_project(table, swapped_in(parts, "ch", 2), order_start, degree_start)
     return gathered.reshape(slab, lblock, -1)
 
 

time: 162 us -> 181 us (1.12)
  local copies, waits for them, and re-layouts: 26.6 us -> 42.5 us
  between operations: 13.6 us -> 0.15 us
  starting transfers between devices: 0.01 us -> 6.95 us
  waiting for transfers between devices: 56.5 us -> 62.2 us
  matrix products: 5.07 us -> 8.55 us
    all_to_all x0 -> x1, waiting for transfers between devices: none -> 62.2 us  [swapped_in(): return jnp.concatenate(lax.all_to_all(stack, axis, 0, 0), axis=along)]
    all_gather x1 -> x0, waiting for transfers between devices: 56.5 us -> none  [shards(): lax.all_gather(parts, 'ch', axis=2, tiled=True)]
    reshape x0 -> x2, local copies, waits for them, and re-layouts: none -> 18.9 us  [swapped_in(): return jnp.concatenate(lax.all_to_all(stack, axis, 0, 0), axis=along)]
    all_to_all x0 -> x1, starting transfers between devices: none -> 6.95 us  [swapped_in(): return jnp.concatenate(lax.all_to_all(stack, axis, 0, 0), axis=along)]
    slice x1 -> x0, local copies, waits for them, and re-layouts: 6.52 us -> none  [parity_project(): parts[:, :hemisphere]]
    another operation x0 -> x1, local copies, waits for them, and re-layouts: none -> 4.27 us  [swapped_in(): stack = jnp.stack([block] * lax.axis_size(axis))]
    dot_general x1, matrix products: 2.01 us -> 3.86 us  [parity_project(): jnp.einsum('mlk,bkcrm->mlbcr', anti_table, parts[:, hemisphere:], preferr...]
    unnamed x9 -> x7, local copies, waits for them, and re-layouts: 4.41 us -> 4.4 us
where the time goes in v1:
time: 181 us
  waiting for transfers between devices  62.2 us (34%)
  local copies, waits for them, and re-layouts  42.5 us (23%)
  blocking collectives  38.8 us (21%)
  other arithmetic  21.5 us (12%)
  matrix products  8.55 us (5%)
  starting transfers between devices  6.95 us (4%)
    all_to_all x1, waiting for transfers between devices, swapped_in(): return jnp.concatenate(lax.all_to_all(stack, axis, 0, 0), axis=along)  62.2 us
    all_to_all x1, blocking collectives, shards(): lax.all_to_all(spectrum, 'lat', split_axis=4, concat_axis=1, tiled=True)  38.8 us
    another operation x1, other arithmetic  19.1 us
    reshape x2, local copies, waits for them, and re-layouts, swapped_in(): return jnp.concatenate(lax.all_to_all(stack, axis, 0, 0), axis=along)  18.9 us
    all_to_all x1, starting transfers between devices, swapped_in(): return jnp.concatenate(lax.all_to_all(stack, axis, 0, 0), axis=along)  6.95 us
    another operation x1, local copies, waits for them, and re-layouts, parity_project(): joined = jnp.stack([first_out, second_out], axis=2)  5.04 us
    unnamed x7, local copies, waits for them, and re-layouts  4.4 us
    another operation x1, local copies, waits for them, and re-layouts, swapped_in(): stack = jnp.stack([block] * lax.axis_size(axis))  4.27 us
  transfers between devices with their start and end apart: 1, of which 1 were waited for; matrix products, arithmetic and copies ran while one was open for 1% of the time, Pallas kernels for 0%

profile of v1, /device:TPU:1, one launch (start us, length us, event | category | flops | bytes accessed | tf_op | source)
XLA Modules:
  0.0 180.7 jit_solution(7924179101784113105)
XLA Ops:
  0.0 0.0 copy-start
  0.0 19.1 %multiply_convert_fusion = (bf16[1440,704]{1,0:T(8,128)(2,1)S(1)}, bf16[1440,704]{1,0:T(8,128)(2,1)S(1)}) fusion(), kind=kLoop, calls=%fused_computation.3 | loop fusion | flops 14192640 | bytes 4055040 | tf_op jit(solution)/shard_map/convert.1
  19.1 0.0 copy-done
  19.1 1.0 fusion.7
  20.2 0.3 reshape.60
  20.5 1.8 %copy.21 = bf16[2,22,2,2,704]{1,3,2,0,4:T(2,128)(2,1)S(1)} copy(bf16[2,22,2,2,704]{4,3,1,2,0:T(2,128)(2,1)S(1)} %reshape.60) | data formatting | bytes 495616 | tf_op jit(solution)/shard_map/reshape | solution.py:53
  22.3 1.8 reshape.61
  24.1 38.8 %all_to_all.23 = bf16[32,2,1936]{2,1,0:T(2,128)(2,1)S(1)} all-to-all(bf16[32,2,1936]{2,1,0:T(2,128)(2,1)S(1)} %reshape.61), channel_id=1, replica_groups=mesh['lat'=32,'ch'=16] {'lat'}, dimensions={0} | all-to-all | bytes 495616 | tf_op jit(solution)/shard_map/all_to_all | solution.py:54
  62.9 1.8 reshape.62
  64.7 0.4 copy.38
  65.1 2.9 %all_to_all.19 = bf16[2,704,2,2,22]{1,3,4,2,0:T(2,128)(2,1)S(1)} reshape(bf16[2,32,22,2,2,22]{2,1,4,5,3,0:T(8,128)(2,1)S(1)} %bitcast.47) | data formatting | bytes 495616 | tf_op jit(solution)/shard_map/all_to_all | solution.py:54
  68.1 0.2 slice.25
  68.3 0.8 reverse
  69.1 0.3 fusion.19
  69.4 0.1 fusion.20
  69.6 0.4 pad_maximum_fusion.1
  70.0 0.2 copy.24
  70.2 4.3 %stack.8 = bf16[16,2,704,2,2,22]{2,3,4,1,5,0:T(2,128)(2,1)} broadcast(bf16[2,704,2,2,22]{1,2,3,0,4:T(2,128)(2,1)S(1)} %copy.24), dimensions={1,2,3,4,5} | broadcast | bytes 4212736 | tf_op jit(solution)/shard_map/stack | solution.py:11
  74.5 0.0 copy-start.1
  74.5 6.9 %all-to-all-start.1 = ((bf16[16,2,704,2,2,22]{2,3,4,1,5,0:T(2,128)(2,1)}), bf16[16,2,704,2,2,22]{2,3,4,1,5,0:T(2,128)(2,1)}, u32[]{:S(2)}, u32[]{:S(2)}) async-start(bf16[16,2,704,2,2,22]{2,3,4,1,5,0:T(2,128)(2,1)} %stack.8), calls=%async_computation.1 | async-start | bytes 8650752 | tf_op jit(solution)/shard_map/all_to_all | solution.py:12
  81.4 0.0 copy-done.1
  81.4 1.0 slice.18
  82.5 1.0 slice.19
  83.6 62.2 %all-to-all-done.1 = bf16[16,2,704,2,2,22]{2,3,4,1,5,0:T(2,128)(2,1)} async-done(((bf16[16,2,704,2,2,22]{2,3,4,1,5,0:T(2,128)(2,1)}), bf16[16,2,704,2,2,22]{2,3,4,1,5,0:T(2,128)(2,1)}, u32[]{:S(2)}, u32[]{:S(2)}) %all-to-all-start.1) | async-done | bytes 3964960 | tf_op jit(solution)/shard_map/all_to_all | solution.py:12
  145.8 9.1 %copy.25 = bf16[2,704,16,2,2,22]{1,3,2,4,0,5:T(2,128)(2,1)} copy(bf16[2,704,16,2,2,22]{1,3,4,0,5,2:T(2,128)(2,1)} %bitcast.8) | data formatting | bytes 7929856 | tf_op jit(solution)/shard_map/reshape | solution.py:12
  154.9 9.8 %reshape.56 = bf16[2,704,32,2,22]{1,2,3,0,4:T(8,128)(2,1)} reshape(bf16[2,704,16,2,2,22]{1,3,2,4,0,5:T(2,128)(2,1)} %copy.25) | data formatting | bytes 7929856 | tf_op jit(solution)/shard_map/reshape | solution.py:12
  164.6 3.9 %fusion.8 = f32[22,22,2,32,2]{3,1,4,2,0:T(8,128)S(1)} fusion(bf16[2,704,32,2,22]{1,2,3,0,4:T(8,128)(2,1)} %reshape.56, bf16[22,22,352]{2,1,0:T(8,128)(2,1)S(1)} %slice.19, bf16[22,22,352]{2,1,0:T(8,128)(2,1)S(1)} %slice.18, pred[22]{0:T(512)(128)(4,1)S(1)} %fusion.21), kind=kOutput, calls=%fused_computation.13 | convolution fusion | flops 43784576 | bytes 3091990 | tf_op jit(solution)/shard_map/mlk,bkcrm->mlbcr/dot_general | solution.py:37
  168.5 3.6 %select_bitcast_fusion.1 = (f32[22,22,1,2,32,2]{4,1,5,3,0,2:T(8,128)S(1)}, f32[22,22,1,2,32,2]{4,1,5,3,0,2:T(8,128)S(1)}) fusion(f32[22,22,2,32,2]{3,1,4,2,0:T(8,128)S(1)} %fusion.8, pred[22]{0:T(512)(128)(4,1)S(1)} %fusion.21, bf16[2,704,32,2,22]{1,2,3,0,4:T(8,128)(2,1)} %reshape.56, bf16[22,22,352]{2,1,0:T(8,128)(2,1)S(1)} %slice.18, ...), kind=kOutput, calls=%fused_computation.20 | convolution fusion | flops 43908480 | bytes 4551680 | tf_op jit(solution)/shard_map/mlk,bkcrm->mlbcr/dot_general | solution.py:34
  172.1 1.6 pad_maximum_fusion
  173.7 5.0 %copy.26 = f32[22,22,2,2,32,2]{0,5,4,3,2,1:T(2,128)S(1)} copy(f32[22,22,2,2,32,2]{4,1,5,3,0,2:T(8,128)} %pad_maximum_fusion) | data formatting | bytes 991232 | tf_op jit(solution)/shard_map/stack | solution.py:43
  178.8 1.9 %copy.27 = f32[22,44,128]{2,1,0:T(8,128)} copy(f32[22,44,128]{0,2,1:T(8,128)S(1)} %bitcast.45) | data formatting | bytes 991232 | tf_op jit(solution)/shard_map/reshape;reshape | solution.py:63
  (1 shorter events, 0.0 us)
Async XLA Ops:
  0.0 19.1 %copy-start = (bf16[2,22,2,1440]{3,2,1,0:T(2,128)(2,1)S(1)}, bf16[2,22,2,1440]{3,2,1,0:T(2,128)(2,1)}, u32[]{:S(2)}) copy-start(bf16[2,22,2,1440]{3,2,1,0:T(2,128)(2,1)} %param.2) | copy-start | bytes 760324
  74.5 7.0 %copy-start.1 = (bf16[22,44,352]{2,1,0:T(8,128)(2,1)S(1)}, bf16[22,44,352]{2,1,0:T(8,128)(2,1)}, u32[]{:S(2)}) copy-start(bf16[22,44,352]{2,1,0:T(8,128)(2,1)} %param.3) | copy-start | bytes 2044420
  74.5 71.3 %all-to-all-start.1 = ((bf16[16,2,704,2,2,22]{2,3,4,1,5,0:T(2,128)(2,1)}), bf16[16,2,704,2,2,22]{2,3,4,1,5,0:T(2,128)(2,1)}, u32[]{:S(2)}, u32[]{:S(2)}) async-start(bf16[16,2,704,2,2,22]{2,3,4,1,5,0:T(2,128)(2,1)} %stack.8), calls=%async_computation.1 | async-start | bytes 8650752 | tf_op jit(solution)/shard_map/all_to_all | solution.py:12
